TPU v7x, 32 devices: a whole 2x2x4 slice. The times are simulated.
32 devices in a mesh: layer: 8 (over z, x), front: 4 (over y, core).
Axes of the slice: x: 2, y: 2, z: 4, core: 2. Of those that a mesh axis runs over, the one named last changes fastest.
Arguments:
- u_factor: bfloat16 [8, 2, 1024, 2560], P('layer', None, None, 'front'), may hold values from -0.1875 to 0.1875
- vt_factor: bfloat16 [8, 2, 1024, 2560], P('layer', None, None, 'front'), may hold values from -0.1875 to 0.1875
- diagonal: float32 [8, 2, 1024], P('layer', None, 'front'), may hold values from 1.5 to 3
- transmit: float32 [8, 1024], P('layer', 'front'), may hold values from 0.3 to 0.97
- sources: float32 [8, 2, 8, 1024], P('layer', None, None, 'front'), may hold values from -6 to 6
Outputs:
- field: float32 [8, 2, 8, 1024], P('layer', None, None, 'front')
All inputs are finite; a program needn't handle non-finite values.
Results may differ from a plain program's by a relative error of at most 0.0003.
Values may be sent and summed in bfloat16 or wider, within the bound.
No kernel may reach another device: no remote copies, remote signals or barrier semaphores. Data moves between devices by JAX's collectives and lax.ppermute only.
A program may use at most 64 MiB of HBM per device.

v0:
```python
import jax
import jax.numpy as jnp
from jax import lax
from jax.sharding import PartitionSpec as P

JACOBI = 3


def passed_along(block, axis, distance):
    devices = range(lax.axis_size(axis))
    route = [(i - distance, i) for i in devices if i - distance in devices]
    return lax.ppermute(block, axis, route)


def block_product(left_real, left_imag, right_real, right_imag):

    def contract(first, second):
        return jnp.einsum("nik,njk->nij", first, second, preferred_element_type=jnp.float32)

    real_part = contract(left_real, right_real) - contract(left_imag, right_imag)
    imag_part = contract(left_real, right_imag) + contract(left_imag, right_real)
    return jnp.stack([real_part, imag_part], axis=1)


def complex_divide(real_num, imag_num, diag_real, diag_imag):
    denominator = diag_real * diag_real + diag_imag * diag_imag
    return (
        (real_num * diag_real + imag_num * diag_imag) / denominator,
        (imag_num * diag_real - real_num * diag_imag) / denominator,
    )


def float_product(form, first, second):
    return jnp.einsum(
        form, first, second, precision=lax.Precision.HIGHEST, preferred_element_type=jnp.float32
    )


def apply_block(block, part_real, part_imag):
    out_real = float_product("ij,rj->ri", block[0], part_real) - float_product(
        "ij,rj->ri", block[1], part_imag
    )
    out_imag = float_product("ij,rj->ri", block[0], part_imag) + float_product(
        "ij,rj->ri", block[1], part_real
    )
    return (out_real, out_imag)


def solve_layer(block, diag_local, gain_local, source_part, incoming):
    diag_real = diag_local[0][None, :]
    diag_imag = diag_local[1][None, :]
    gain = gain_local[None, :]
    drive_real = source_part[0] + gain * (diag_real * incoming[0] - diag_imag * incoming[1])
    drive_imag = source_part[1] + gain * (diag_real * incoming[1] + diag_imag * incoming[0])
    state_real, state_imag = complex_divide(drive_real, drive_imag, diag_real, diag_imag)
    for sweep_count in range(JACOBI):
        mixed_real, mixed_imag = apply_block(block, state_real, state_imag)
        state_real, state_imag = complex_divide(
            drive_real + mixed_real, drive_imag + mixed_imag, diag_real, diag_imag
        )
    return jnp.stack([state_real, state_imag], axis=0)


def shards(u_factor, vt_factor, diagonal, transmit, sources):
    cells = diagonal.shape[2]
    left = u_factor[0]
    right = vt_factor[0]
    inner = left.shape[2]
    left = left.reshape(2, 1 * lax.axis_size("front"), cells, inner)
    right = right.reshape(2, 1 * lax.axis_size("front"), cells, inner)
    merged = lax.psum_scatter(
        block_product(left[0], left[1], right[0], right[1]),
        "front",
        scatter_dimension=0,
        tiled=True,
    )
    block = merged[0]
    diag_local = diagonal[0]
    gain_local = transmit[0]
    source_local = sources[0]
    rhs_count = source_local.shape[1]
    layer_place = lax.axis_index("layer")
    layer_count = lax.axis_size("layer")

    def full_turn(turn_index, current):
        incoming = passed_along(current, "layer", 1)
        fresh = solve_layer(block, diag_local, gain_local, source_local, incoming)
        return jnp.where(turn_index == layer_place, fresh, current)

    swept = lax.fori_loop(0, layer_count, full_turn, jnp.zeros((2, rhs_count, cells), jnp.float32))
    return swept[None]


def solution(mesh):
    placed = (
        P("layer", None, None, "front"),
        P("layer", None, None, "front"),
        P("layer", None, "front"),
        P("layer", "front"),
        P("layer", None, None, "front"),
    )
    return jax.shard_map(
        shards,
        mesh=mesh,
        in_specs=placed,
        out_specs=P("layer", None, None, "front"),
        check_vma=False,
    )
```

profile of v0, /device:TPU:24, one launch (start us, length us, event | category | flops | bytes accessed | tf_op | source)
XLA Modules:
  0.0 159.1 jit_solution(7384200557685762816)
XLA Ops:
  6.5 2.1 %fusion.49 = (bf16[1,1,1024,640]{3,2,1,0:T(8,128)(2,1)S(1)}, bf16[1,1,1024,640]{3,2,1,0:T(8,128)(2,1)S(1)}) fusion(bf16[1,2,1024,640]{3,2,1,0:T(8,128)(2,1)} %param.7), kind=kLoop, calls=%fused_computation.77 | loop fusion | bytes 5242880 | tf_op jit(solution)/shard_map/slice | solution.py:72
  8.6 0.4 copy-done
  9.3 0.6 fusion.52
  9.9 0.6 fusion.53
  10.5 0.6 fusion.46
  11.1 0.6 fusion.45
  11.7 1.5 pad_maximum_fusion
  13.3 0.6 copy-done.5
  13.9 0.6 dynamic-slice
  14.5 51.3 %all-reduce.3.cloned.1.call-done = f32[4,2,256,256]{3,2,0,1:T(8,128)} async-done(((f32[4,2,256,256]{3,2,0,1:T(8,128)}), f32[4,2,256,256]{3,2,0,1:T(8,128)}) %all-reduce.3.cloned.1.call-update) | async-done | bytes 2097168
  65.8 1.7 %dynamic-slice_bitcast_fusion = f32[2,256,256]{2,1,0:T(8,128)S(1)} fusion(f32[4,2,256,256]{3,2,0,1:T(8,128)} %all-reduce.3.cloned.1.call-done, u32[]{:T(128)} %bitcast.31), kind=kLoop, calls=%fused_computation.73 | loop fusion | bytes 1048580 | tf_op jit(solution)/shard_map/squeeze | solution.py:77
  67.5 84.2 %while.16 = (s32[]{:T(128)}, f32[2,8,256]{2,1,0:T(8,128)S(1)}, s32[]{:T(128)}, f32[2,8,256]{2,1,0:T(8,128)S(1)}, f32[1,256]{1,0:T(1,128)S(1)}, /*index=5*/f32[2,...) while((s32[]{:T(128)}, f32[2,8,256]{2,1,0:T(8,128)S(1)}, ...), condition=%wide.region_2.3_spmd.clone, body=%wide.region_1.2_spmd.clone.sunk | while | flops 75677696 | bytes 3807394 | solution.py:90
  67.5 3.4 %collective-permute-start = (f32[2,8,256]{2,1,0:T(8,128)S(1)}, f32[2,8,256]{2,1,0:T(8,128)S(1)}, u32[]{:S(2)}, u32[]{:S(2)}) collective-permute-start(f32[2,8,256]{2,1,0:T(8,128)S(1)} %broadcast_select_fusion.2), channel_id=1, source_target_pairs={{0,4},{4,8},{8,12},{12,16},{16,20},{20,24},{24,28},{1,5},{5,9},{9,... | collective-permute-start | bytes 49160 | tf_op jit(solution)/shard_map/while/body/eval_jaxpr/ppermute | solution.py:12
  70.9 3.1 %collective-permute-done = f32[2,8,256]{2,1,0:T(8,128)S(1)} collective-permute-done((f32[2,8,256]{2,1,0:T(8,128)S(1)}, f32[2,8,256]{2,1,0:T(8,128)S(1)}, u32[]{:S(2)}, u32[]{:S(2)}) %collective-permute-start) | collective-permute-done | bytes 16416 | tf_op jit(solution)/shard_map/while/body/eval_jaxpr/ppermute | solution.py:12
  75.0 0.3 fusion.108
  76.0 0.3 fusion.114
  76.3 0.3 fusion.112
  77.3 0.3 fusion.116
  77.6 0.4 divide_bitcast_fusion.3
  78.0 2.5 %collective-permute-start = (f32[2,8,256]{2,1,0:T(8,128)S(1)}, f32[2,8,256]{2,1,0:T(8,128)S(1)}, u32[]{:S(2)}, u32[]{:S(2)}) collective-permute-start(f32[2,8,256]{2,1,0:T(8,128)S(1)} %broadcast_select_fusion.2), channel_id=1, source_target_pairs={{0,4},{4,8},{8,12},{12,16},{16,20},{20,24},{24,28},{1,5},{5,9},{9,... | collective-permute-start | bytes 49160 | tf_op jit(solution)/shard_map/while/body/eval_jaxpr/ppermute | solution.py:12
  80.5 4.0 %collective-permute-done = f32[2,8,256]{2,1,0:T(8,128)S(1)} collective-permute-done((f32[2,8,256]{2,1,0:T(8,128)S(1)}, f32[2,8,256]{2,1,0:T(8,128)S(1)}, u32[]{:S(2)}, u32[]{:S(2)}) %collective-permute-start) | collective-permute-done | bytes 16416 | tf_op jit(solution)/shard_map/while/body/eval_jaxpr/ppermute | solution.py:12
  85.5 0.3 fusion.108
  86.5 0.3 fusion.114
  86.8 0.3 fusion.112
  87.8 0.3 fusion.116
  88.1 0.4 divide_bitcast_fusion.3
  88.6 1.9 %collective-permute-start = (f32[2,8,256]{2,1,0:T(8,128)S(1)}, f32[2,8,256]{2,1,0:T(8,128)S(1)}, u32[]{:S(2)}, u32[]{:S(2)}) collective-permute-start(f32[2,8,256]{2,1,0:T(8,128)S(1)} %broadcast_select_fusion.2), channel_id=1, source_target_pairs={{0,4},{4,8},{8,12},{12,16},{16,20},{20,24},{24,28},{1,5},{5,9},{9,... | collective-permute-start | bytes 49160 | tf_op jit(solution)/shard_map/while/body/eval_jaxpr/ppermute | solution.py:12
  90.5 4.6 %collective-permute-done = f32[2,8,256]{2,1,0:T(8,128)S(1)} collective-permute-done((f32[2,8,256]{2,1,0:T(8,128)S(1)}, f32[2,8,256]{2,1,0:T(8,128)S(1)}, u32[]{:S(2)}, u32[]{:S(2)}) %collective-permute-start) | collective-permute-done | bytes 16416 | tf_op jit(solution)/shard_map/while/body/eval_jaxpr/ppermute | solution.py:12
  96.0 0.3 fusion.108
  97.0 0.3 fusion.114
  97.3 0.3 fusion.112
  98.3 0.3 fusion.116
  98.6 0.4 divide_bitcast_fusion.3
  99.1 1.9 %collective-permute-start = (f32[2,8,256]{2,1,0:T(8,128)S(1)}, f32[2,8,256]{2,1,0:T(8,128)S(1)}, u32[]{:S(2)}, u32[]{:S(2)}) collective-permute-start(f32[2,8,256]{2,1,0:T(8,128)S(1)} %broadcast_select_fusion.2), channel_id=1, source_target_pairs={{0,4},{4,8},{8,12},{12,16},{16,20},{20,24},{24,28},{1,5},{5,9},{9,... | collective-permute-start | bytes 49160 | tf_op jit(solution)/shard_map/while/body/eval_jaxpr/ppermute | solution.py:12
  101.0 4.6 %collective-permute-done = f32[2,8,256]{2,1,0:T(8,128)S(1)} collective-permute-done((f32[2,8,256]{2,1,0:T(8,128)S(1)}, f32[2,8,256]{2,1,0:T(8,128)S(1)}, u32[]{:S(2)}, u32[]{:S(2)}) %collective-permute-start) | collective-permute-done | bytes 16416 | tf_op jit(solution)/shard_map/while/body/eval_jaxpr/ppermute | solution.py:12
  107.5 0.3 fusion.114
  107.9 0.3 fusion.112
  108.8 0.3 fusion.116
  109.2 0.4 divide_bitcast_fusion.3
  109.6 1.9 %collective-permute-start = (f32[2,8,256]{2,1,0:T(8,128)S(1)}, f32[2,8,256]{2,1,0:T(8,128)S(1)}, u32[]{:S(2)}, u32[]{:S(2)}) collective-permute-start(f32[2,8,256]{2,1,0:T(8,128)S(1)} %broadcast_select_fusion.2), channel_id=1, source_target_pairs={{0,4},{4,8},{8,12},{12,16},{16,20},{20,24},{24,28},{1,5},{5,9},{9,... | collective-permute-start | bytes 49160 | tf_op jit(solution)/shard_map/while/body/eval_jaxpr/ppermute | solution.py:12
  111.5 4.6 %collective-permute-done = f32[2,8,256]{2,1,0:T(8,128)S(1)} collective-permute-done((f32[2,8,256]{2,1,0:T(8,128)S(1)}, f32[2,8,256]{2,1,0:T(8,128)S(1)}, u32[]{:S(2)}, u32[]{:S(2)}) %collective-permute-start) | collective-permute-done | bytes 16416 | tf_op jit(solution)/shard_map/while/body/eval_jaxpr/ppermute | solution.py:12
  118.0 0.3 fusion.114
  118.4 0.3 fusion.112
  119.4 0.3 fusion.116
  119.7 0.4 divide_bitcast_fusion.3
  120.1 1.9 %collective-permute-start = (f32[2,8,256]{2,1,0:T(8,128)S(1)}, f32[2,8,256]{2,1,0:T(8,128)S(1)}, u32[]{:S(2)}, u32[]{:S(2)}) collective-permute-start(f32[2,8,256]{2,1,0:T(8,128)S(1)} %broadcast_select_fusion.2), channel_id=1, source_target_pairs={{0,4},{4,8},{8,12},{12,16},{16,20},{20,24},{24,28},{1,5},{5,9},{9,... | collective-permute-start | bytes 49160 | tf_op jit(solution)/shard_map/while/body/eval_jaxpr/ppermute | solution.py:12
  122.1 4.6 %collective-permute-done = f32[2,8,256]{2,1,0:T(8,128)S(1)} collective-permute-done((f32[2,8,256]{2,1,0:T(8,128)S(1)}, f32[2,8,256]{2,1,0:T(8,128)S(1)}, u32[]{:S(2)}, u32[]{:S(2)}) %collective-permute-start) | collective-permute-done | bytes 16416 | tf_op jit(solution)/shard_map/while/body/eval_jaxpr/ppermute | solution.py:12
  128.6 0.3 fusion.114
  128.9 0.3 fusion.112
  129.9 0.3 fusion.116
  130.2 0.4 divide_bitcast_fusion.3
  130.6 1.9 %collective-permute-start = (f32[2,8,256]{2,1,0:T(8,128)S(1)}, f32[2,8,256]{2,1,0:T(8,128)S(1)}, u32[]{:S(2)}, u32[]{:S(2)}) collective-permute-start(f32[2,8,256]{2,1,0:T(8,128)S(1)} %broadcast_select_fusion.2), channel_id=1, source_target_pairs={{0,4},{4,8},{8,12},{12,16},{16,20},{20,24},{24,28},{1,5},{5,9},{9,... | collective-permute-start | bytes 49160 | tf_op jit(solution)/shard_map/while/body/eval_jaxpr/ppermute | solution.py:12
  132.6 4.6 %collective-permute-done = f32[2,8,256]{2,1,0:T(8,128)S(1)} collective-permute-done((f32[2,8,256]{2,1,0:T(8,128)S(1)}, f32[2,8,256]{2,1,0:T(8,128)S(1)}, u32[]{:S(2)}, u32[]{:S(2)}) %collective-permute-start) | collective-permute-done | bytes 16416 | tf_op jit(solution)/shard_map/while/body/eval_jaxpr/ppermute | solution.py:12
  139.1 0.3 fusion.114
  139.4 0.3 fusion.112
  140.4 0.3 fusion.116
  140.7 0.4 divide_bitcast_fusion.3
  141.2 1.9 %collective-permute-start = (f32[2,8,256]{2,1,0:T(8,128)S(1)}, f32[2,8,256]{2,1,0:T(8,128)S(1)}, u32[]{:S(2)}, u32[]{:S(2)}) collective-permute-start(f32[2,8,256]{2,1,0:T(8,128)S(1)} %broadcast_select_fusion.2), channel_id=1, source_target_pairs={{0,4},{4,8},{8,12},{12,16},{16,20},{20,24},{24,28},{1,5},{5,9},{9,... | collective-permute-start | bytes 49160 | tf_op jit(solution)/shard_map/while/body/eval_jaxpr/ppermute | solution.py:12
  143.1 4.6 %collective-permute-done = f32[2,8,256]{2,1,0:T(8,128)S(1)} collective-permute-done((f32[2,8,256]{2,1,0:T(8,128)S(1)}, f32[2,8,256]{2,1,0:T(8,128)S(1)}, u32[]{:S(2)}, u32[]{:S(2)}) %collective-permute-start) | collective-permute-done | bytes 16416 | tf_op jit(solution)/shard_map/while/body/eval_jaxpr/ppermute | solution.py:12
  149.6 0.3 fusion.114
  149.9 0.3 fusion.112
  150.9 0.3 fusion.116
  151.2 0.4 divide_bitcast_fusion.3
  151.7 0.6 copy-done.2
  (115 shorter events, 19.9 us)
Async XLA Ops:
  6.5 2.5 %copy-start = (bf16[1,2,1024,640]{3,2,1,0:T(8,128)(2,1)S(1)}, bf16[1,2,1024,640]{3,2,1,0:T(8,128)(2,1)}, u32[]{:S(2)}) copy-start(bf16[1,2,1024,640]{3,2,1,0:T(8,128)(2,1)} %param.8) | copy-start | bytes 7864324
  6.5 59.3 %all-reduce.3.cloned.1.call-start = ((), (), s32[]{:S(2)}) async-start(), calls=%async_computation | async-start | bytes 4194304
  13.3 0.7 copy-start.5
  13.3 1.2 copy-start.4
  13.3 54.2 %copy-start.1 = (f32[1,2,8,256]{3,2,1,0:T(8,128)S(1)}, f32[1,2,8,256]{3,2,1,0:T(8,128)}, u32[]{:S(2)}) copy-start(f32[1,2,8,256]{3,2,1,0:T(8,128)} %param.11) | copy-start | bytes 49156
  13.3 54.2 %copy-start.3 = (f32[1,256]{1,0:T(1,128)S(1)}, f32[1,256]{1,0:T(1,128)}, u32[]{:S(2)}) copy-start(f32[1,256]{1,0:T(1,128)} %param.10) | copy-start | bytes 3076
  67.5 6.5 %collective-permute-start = (f32[2,8,256]{2,1,0:T(8,128)S(1)}, f32[2,8,256]{2,1,0:T(8,128)S(1)}, u32[]{:S(2)}, u32[]{:S(2)}) collective-permute-start(f32[2,8,256]{2,1,0:T(8,128)S(1)} %broadcast_select_fusion.2), channel_id=1, source_target_pairs={{0,4},{4,8},{8,12},{12,16},{16,20},{20,24},{24,28},{1,5},{5,9},{9,... | collective-permute-start | bytes 49160 | tf_op jit(solution)/shard_map/while/body/eval_jaxpr/ppermute | solution.py:12
  78.0 6.5 %collective-permute-start = (f32[2,8,256]{2,1,0:T(8,128)S(1)}, f32[2,8,256]{2,1,0:T(8,128)S(1)}, u32[]{:S(2)}, u32[]{:S(2)}) collective-permute-start(f32[2,8,256]{2,1,0:T(8,128)S(1)} %broadcast_select_fusion.2), channel_id=1, source_target_pairs={{0,4},{4,8},{8,12},{12,16},{16,20},{20,24},{24,28},{1,5},{5,9},{9,... | collective-permute-start | bytes 49160 | tf_op jit(solution)/shard_map/while/body/eval_jaxpr/ppermute | solution.py:12
  88.6 6.5 %collective-permute-start = (f32[2,8,256]{2,1,0:T(8,128)S(1)}, f32[2,8,256]{2,1,0:T(8,128)S(1)}, u32[]{:S(2)}, u32[]{:S(2)}) collective-permute-start(f32[2,8,256]{2,1,0:T(8,128)S(1)} %broadcast_select_fusion.2), channel_id=1, source_target_pairs={{0,4},{4,8},{8,12},{12,16},{16,20},{20,24},{24,28},{1,5},{5,9},{9,... | collective-permute-start | bytes 49160 | tf_op jit(solution)/shard_map/while/body/eval_jaxpr/ppermute | solution.py:12
  99.1 6.5 %collective-permute-start = (f32[2,8,256]{2,1,0:T(8,128)S(1)}, f32[2,8,256]{2,1,0:T(8,128)S(1)}, u32[]{:S(2)}, u32[]{:S(2)}) collective-permute-start(f32[2,8,256]{2,1,0:T(8,128)S(1)} %broadcast_select_fusion.2), channel_id=1, source_target_pairs={{0,4},{4,8},{8,12},{12,16},{16,20},{20,24},{24,28},{1,5},{5,9},{9,... | collective-permute-start | bytes 49160 | tf_op jit(solution)/shard_map/while/body/eval_jaxpr/ppermute | solution.py:12
  109.6 6.5 %collective-permute-start = (f32[2,8,256]{2,1,0:T(8,128)S(1)}, f32[2,8,256]{2,1,0:T(8,128)S(1)}, u32[]{:S(2)}, u32[]{:S(2)}) collective-permute-start(f32[2,8,256]{2,1,0:T(8,128)S(1)} %broadcast_select_fusion.2), channel_id=1, source_target_pairs={{0,4},{4,8},{8,12},{12,16},{16,20},{20,24},{24,28},{1,5},{5,9},{9,... | collective-permute-start | bytes 49160 | tf_op jit(solution)/shard_map/while/body/eval_jaxpr/ppermute | solution.py:12
  120.1 6.5 %collective-permute-start = (f32[2,8,256]{2,1,0:T(8,128)S(1)}, f32[2,8,256]{2,1,0:T(8,128)S(1)}, u32[]{:S(2)}, u32[]{:S(2)}) collective-permute-start(f32[2,8,256]{2,1,0:T(8,128)S(1)} %broadcast_select_fusion.2), channel_id=1, source_target_pairs={{0,4},{4,8},{8,12},{12,16},{16,20},{20,24},{24,28},{1,5},{5,9},{9,... | collective-permute-start | bytes 49160 | tf_op jit(solution)/shard_map/while/body/eval_jaxpr/ppermute | solution.py:12
  130.6 6.5 %collective-permute-start = (f32[2,8,256]{2,1,0:T(8,128)S(1)}, f32[2,8,256]{2,1,0:T(8,128)S(1)}, u32[]{:S(2)}, u32[]{:S(2)}) collective-permute-start(f32[2,8,256]{2,1,0:T(8,128)S(1)} %broadcast_select_fusion.2), channel_id=1, source_target_pairs={{0,4},{4,8},{8,12},{12,16},{16,20},{20,24},{24,28},{1,5},{5,9},{9,... | collective-permute-start | bytes 49160 | tf_op jit(solution)/shard_map/while/body/eval_jaxpr/ppermute | solution.py:12
  141.2 6.5 %collective-permute-start = (f32[2,8,256]{2,1,0:T(8,128)S(1)}, f32[2,8,256]{2,1,0:T(8,128)S(1)}, u32[]{:S(2)}, u32[]{:S(2)}) collective-permute-start(f32[2,8,256]{2,1,0:T(8,128)S(1)} %broadcast_select_fusion.2), channel_id=1, source_target_pairs={{0,4},{4,8},{8,12},{12,16},{16,20},{20,24},{24,28},{1,5},{5,9},{9,... | collective-permute-start | bytes 49160 | tf_op jit(solution)/shard_map/while/body/eval_jaxpr/ppermute | solution.py:12
  151.7 0.6 copy-start.2
Sparse Core Ops, SparseCore 0:
  13.4 52.3 all-reduce.2
where the time goes:
time: 160 us; the launch traced here: 159 us
  waiting for transfers between devices  86 us (54%)
  matrix products  33.1 us (21%)
  starting transfers between devices  17.4 us (11%)
  between operations  13.5 us (8%)
  local copies, waits for them, and re-layouts  6.23 us (4%)
  other arithmetic  2.27 us (1%)
    unnamed x2, waiting for transfers between devices  51.3 us
    ppermute x8, waiting for transfers between devices, passed_along(): return lax.ppermute(block, axis, route)  34.7 us
    dot_general x96, matrix products, float_product(): jnp.einsum(form, first, second, precision=lax.Precision.HIGHEST, preferre...  30.7 us
    ppermute x8, starting transfers between devices, passed_along(): return lax.ppermute(block, axis, route)  17.4 us
  transfers between devices with their start and end apart: 9, of which 9 were waited for; matrix products, arithmetic and copies ran while one was open for 0% of the time, Pallas kernels for 0%

commit v1 on v0

v1 whole, which is shorter than its diff:
```python
import functools

import jax
import jax.numpy as jnp
from jax import lax
from jax.experimental import pallas as pl
from jax.experimental.pallas import tpu as pltpu
from jax.sharding import PartitionSpec as P

JACOBI = 3
LINK = jnp.float16
VMEM = pl.BlockSpec(memory_space=pltpu.VMEM)


def swapped(value, axis, mask):
    route = [(i, i ^ mask) for i in range(lax.axis_size(axis))]
    return lax.ppermute(value, axis, route)


def products_kernel(masks, u_hbm, vt_hbm, out_ref, u_buf, vt_buf, sems):
    me = lax.axis_index("front")
    cells = u_buf.shape[2]
    copies = []
    for place, mask in enumerate(masks):
        group = jnp.bitwise_xor(me, mask)
        rows = pl.ds(pl.multiple_of(group * cells, cells), cells)
        pair = (
            pltpu.make_async_copy(u_hbm.at[0, :, rows, :], u_buf.at[place], sems.at[0, place]),
            pltpu.make_async_copy(vt_hbm.at[0, :, rows, :], vt_buf.at[place], sems.at[1, place]),
        )
        for copy in pair:
            copy.start()
        copies.append(pair)

    def contract(first, second):
        return lax.dot_general(
            first, second, (((1,), (1,)), ((), ())), preferred_element_type=jnp.float32
        )

    for place, pair in enumerate(copies):
        for copy in pair:
            copy.wait()
        u_real, u_imag = u_buf[place, 0], u_buf[place, 1]
        v_real, v_imag = vt_buf[place, 0], vt_buf[place, 1]
        out_ref[place, 0] = contract(v_real, u_real) - contract(v_imag, u_imag)
        out_ref[place, 1] = contract(v_real, u_imag) + contract(v_imag, u_real)


def products(u_factor, vt_factor, masks, cells):
    inner = u_factor.shape[3]
    count = len(masks)
    return pl.pallas_call(
        functools.partial(products_kernel, masks),
        out_shape=jax.ShapeDtypeStruct((count, 2, cells, cells), jnp.float32),
        in_specs=[pl.BlockSpec(memory_space=pltpu.HBM)] * 2,
        out_specs=VMEM,
        scratch_shapes=[
            pltpu.VMEM((count, 2, cells, inner), u_factor.dtype),
            pltpu.VMEM((count, 2, cells, inner), vt_factor.dtype),
            pltpu.SemaphoreType.DMA((2, count)),
        ],
        compiler_params=pltpu.CompilerParams(vmem_limit_bytes=24 << 20),
        cost_estimate=pl.CostEstimate(
            flops=8 * count * cells * cells * inner,
            bytes_accessed=count * cells * (8 * inner + 8 * cells),
            transcendentals=0,
        ),
        name="products",
    )(u_factor, vt_factor)


def apply_block(high_ref, low_ref, real, imag):
    count, cells = real.shape
    state = jnp.concatenate([real, imag], axis=0)
    top = state.astype(jnp.bfloat16)
    rest = (state - top.astype(jnp.float32)).astype(jnp.bfloat16)
    both = jnp.concatenate([top, rest], axis=0)
    by_high = jnp.dot(both, high_ref[...], preferred_element_type=jnp.float32)
    by_low = jnp.dot(top, low_ref[...], preferred_element_type=jnp.float32)
    total = by_high[: 2 * count] + by_high[2 * count :] + by_low
    return (
        total[:count, :cells] - total[count:, cells:],
        total[:count, cells:] + total[count:, :cells],
    )


def solve(high_ref, low_ref, small, incoming):
    rhs = (small.shape[0] - 8) // 2
    diag_real = small[2 * rhs : 2 * rhs + 1]
    diag_imag = small[2 * rhs + 1 : 2 * rhs + 2]
    gain = small[2 * rhs + 2 : 2 * rhs + 3]
    scale = 1.0 / (diag_real * diag_real + diag_imag * diag_imag)
    inv_real, inv_imag = diag_real * scale, -diag_imag * scale
    h_real, h_imag = small[:rhs], small[rhs : 2 * rhs]
    if incoming is not None:
        in_real, in_imag = incoming
        h_real = h_real + gain * (diag_real * in_real - diag_imag * in_imag)
        h_imag = h_imag + gain * (diag_real * in_imag + diag_imag * in_real)

    def divided(real, imag):
        return real * inv_real - imag * inv_imag, real * inv_imag + imag * inv_real

    x_real, x_imag = divided(h_real, h_imag)
    for _ in range(JACOBI):
        mixed_real, mixed_imag = apply_block(high_ref, low_ref, x_real, x_imag)
        x_real, x_imag = divided(h_real + mixed_real, h_imag + mixed_imag)
    return x_real, x_imag


def both_layers(blocks_ref, small_ref, incoming, out_ref):
    first = solve(blocks_ref.at[0], blocks_ref.at[1], small_ref[0], incoming)
    second = solve(blocks_ref.at[2], blocks_ref.at[3], small_ref[1], first)
    out_ref[0, 0], out_ref[0, 1] = first
    out_ref[1, 0], out_ref[1, 1] = second


def start_kernel(own_ref, other_ref, small_own, small_partner, blocks_ref, small_ref, out_ref):
    odd = lax.rem(lax.axis_index("layer"), 2) == 1
    cells = own_ref.shape[1]
    for part in range(2):
        own, other = own_ref[part], other_ref[part]
        columns = slice(part * cells, (part + 1) * cells)
        for place, block in enumerate((jnp.where(odd, other, own), jnp.where(odd, own, other))):
            high = block.astype(jnp.bfloat16)
            blocks_ref[2 * place, :, columns] = high
            blocks_ref[2 * place + 1, :, columns] = (block - high.astype(jnp.float32)).astype(
                jnp.bfloat16
            )
    small_ref[0] = jnp.where(odd, small_partner[...], small_own[...])
    small_ref[1] = jnp.where(odd, small_own[...], small_partner[...])
    both_layers(blocks_ref, small_ref, None, out_ref)


def hop_kernel(hop, blocks_ref, small_ref, came, current, out_ref):
    pair = lax.axis_index("layer") // 2

    @pl.when(pair == hop)
    def _():
        both_layers(blocks_ref, small_ref, (came[0], came[1]), out_ref)

    @pl.when(pair != hop)
    def _():
        out_ref[...] = current[...]


def shards(u_factor, vt_factor, diagonal, transmit, sources):
    cells = diagonal.shape[2]
    rhs = sources.shape[2]
    fronts = lax.axis_size("front")
    layers = lax.axis_size("layer")
    limit = pltpu.CompilerParams(vmem_limit_bytes=16 << 20)

    small_own = jnp.concatenate(
        [
            sources[0].reshape(2 * rhs, cells),
            diagonal[0],
            transmit,
            jnp.zeros((5, cells), jnp.float32),
        ],
        axis=0,
    )
    small_partner = swapped(small_own, "layer", 1)

    half = fronts // 2
    masks = list(range(half, fronts)), list(range(half))
    far = products(u_factor, vt_factor, masks[0], cells)
    near = products(u_factor, vt_factor, masks[1], cells)
    terms = {m: far[i] for i, m in enumerate(masks[0])}
    terms.update({m: near[i] for i, m in enumerate(masks[1])})
    for m in range(fronts - 1, -1, -1):
        if m & 1:
            terms[m ^ 1] = terms[m ^ 1] + swapped(terms[m], "front", 1)
    bit = half
    arrived = None
    while bit > 1:
        for m in range(0, bit, 2):
            arrived = swapped(terms[m + bit].astype(LINK), "front", bit)
            if bit > 2 or m:
                terms[m] = terms[m] + arrived.astype(jnp.float32)
        bit //= 2
    own = terms[0] + arrived.astype(jnp.float32)
    other = swapped(own.astype(LINK), "layer", 1).astype(jnp.float32)

    blocks, small, fields = pl.pallas_call(
        start_kernel,
        out_shape=(
            jax.ShapeDtypeStruct((4, cells, 2 * cells), jnp.bfloat16),
            jax.ShapeDtypeStruct((2,) + small_own.shape, jnp.float32),
            jax.ShapeDtypeStruct((2, 2, rhs, cells), jnp.float32),
        ),
        in_specs=[VMEM] * 4,
        out_specs=(VMEM,) * 3,
        compiler_params=limit,
        name="start",
    )(own, other, small_own, small_partner)

    for hop in range(1, layers // 2):
        route = [(2 * hop - 2 + x, 2 * hop + x) for x in range(2)]
        came = lax.ppermute(fields[1], "layer", route)
        fields = pl.pallas_call(
            functools.partial(hop_kernel, hop),
            out_shape=jax.ShapeDtypeStruct((2, 2, rhs, cells), jnp.float32),
            in_specs=[VMEM] * 4,
            out_specs=VMEM,
            compiler_params=limit,
            name=f"hop{hop}",
        )(blocks, small, came, fields)
    odd = lax.rem(lax.axis_index("layer"), 2) == 1
    return jnp.where(odd, fields[1], fields[0])[None]


def solution(mesh):
    placed = (
        P("layer", None, None, "front"),
        P("layer", None, None, "front"),
        P("layer", None, "front"),
        P("layer", "front"),
        P("layer", None, None, "front"),
    )
    return jax.shard_map(
        shards,
        mesh=mesh,
        in_specs=placed,
        out_specs=P("layer", None, None, "front"),
        check_vma=False,
    )
```

time: 160 us -> 41.8 us (0.26)
  waiting for transfers between devices: 86 us -> 24.2 us
  matrix products: 33.1 us -> 0 us
  between operations: 13.5 us -> 0.18 us
  starting transfers between devices: 17.4 us -> 6.96 us
  Pallas kernels: 0 us -> 5.7 us
  local copies, waits for them, and re-layouts: 6.23 us -> 3.66 us
    unnamed x2 -> x0, waiting for transfers between devices: 51.3 us -> none
    dot_general x100 -> x0, matrix products: 33.1 us -> none  [the longest x96 30.7 us: float_product(): jnp.einsum(form, first, second, precision=lax.Precision.HIGHEST, preferre...]
    ppermute x8, waiting for transfers between devices: 34.7 us -> 24.2 us  [the longest x5 12.4 us: swapped(): return lax.ppermute(value, axis, route)]
    ppermute x8, starting transfers between devices: 17.4 us -> 6.96 us  [the longest x5 4.34 us: swapped(): return lax.ppermute(value, axis, route)]
    pallas_call x0 -> x6, Pallas kernels: none -> 5.7 us  [the longest x2 3.62 us: products(): pl.pallas_call(functools.partial(products_kernel, masks), out_shape=jax.S...]
    slice x10 -> x0, local copies, waits for them, and re-layouts: 2.35 us -> none  [the longest x1 2.09 us: shards(): left[1]]
    unnamed x13 -> x10, local copies, waits for them, and re-layouts: 2.23 us -> 3.5 us
  transfers between devices with their start and end apart: 9 -> 8, of which waited for: 9 -> 4; matrix products, arithmetic and copies ran while one was open for 0% -> 1% of each run, Pallas kernels for 0% -> 4%
where the time goes in v1:
time: 41.8 us; the launch traced here: 41.6 us
  waiting for transfers between devices  24.2 us (58%)
  starting transfers between devices  6.96 us (17%)
  Pallas kernels  5.7 us (14%)
  local copies, waits for them, and re-layouts  3.66 us (9%)
  other arithmetic  0.92 us (2%)
    ppermute x5, waiting for transfers between devices, swapped(): return lax.ppermute(value, axis, route)  12.4 us
    ppermute x3, waiting for transfers between devices, shards(): came = lax.ppermute(fields[1], 'layer', route)  11.8 us
    ppermute x5, starting transfers between devices, swapped(): return lax.ppermute(value, axis, route)  4.34 us
    pallas_call x2, Pallas kernels, products(): pl.pallas_call(functools.partial(products_kernel, masks), out_shape=jax.S...  3.62 us
    unnamed x10, local copies, waits for them, and re-layouts  3.5 us
    ppermute x3, starting transfers between devices, shards(): came = lax.ppermute(fields[1], 'layer', route)  2.62 us
    pallas_call x1, Pallas kernels, shards(): pl.pallas_call(start_kernel, out_shape=(jax.ShapeDtypeStruct((4, cells, 2...  1.04 us
    pallas_call x3, Pallas kernels, shards(): pl.pallas_call(functools.partial(hop_kernel, hop), out_shape=jax.ShapeDty...  1.04 us
  transfers between devices with their start and end apart: 8, of which 4 were waited for; matrix products, arithmetic and copies ran while one was open for 1% of the time, Pallas kernels for 4%

profile of v1, /device:TPU:24, one launch (start us, length us, event | category | flops | bytes accessed | tf_op | source)
XLA Modules:
  0.0 41.6 jit_solution(7744213610706804128)
XLA Ops:
  0.0 0.0 copy-start
  0.0 1.7 %copy-done = bf16[1,2,1024,640]{3,2,1,0:T(8,128)(2,1)S(1)} copy-done((bf16[1,2,1024,640]{3,2,1,0:T(8,128)(2,1)S(1)}, bf16[1,2,1024,640]{3,2,1,0:T(8,128)(2,1)}, u32[]{:S(2)}) %copy-start) | copy-done | bytes 2621464
  1.7 0.0 copy-start.1
  1.7 1.7 %copy-done.1 = bf16[1,2,1024,640]{3,2,1,0:T(8,128)(2,1)S(1)} copy-done((bf16[1,2,1024,640]{3,2,1,0:T(8,128)(2,1)S(1)}, bf16[1,2,1024,640]{3,2,1,0:T(8,128)(2,1)}, u32[]{:S(2)}) %copy-start.1) | copy-done | bytes 2621464
  3.5 1.8 %products.3 = f32[2,2,256,256]{3,2,1,0:T(8,128)S(1)} custom-call(bf16[1,2,1024,640]{3,2,1,0:T(8,128)(2,1)S(1)} %copy-done, bf16[1,2,1024,640]{3,2,1,0:T(8,128)(2,1)S(1)} %copy-done.1), custom_call_target="tpu_custom_call" | custom-call | flops 671088640 | bytes 3670016 | tf_op jit(solution)/shard_map/products/pallas_call | solution.py:52
  5.3 0.1 collective-permute-start.1
  5.4 1.8 %products.2 = f32[2,2,256,256]{3,2,1,0:T(8,128)S(1)} custom-call(bf16[1,2,1024,640]{3,2,1,0:T(8,128)(2,1)S(1)} %copy-done, bf16[1,2,1024,640]{3,2,1,0:T(8,128)(2,1)S(1)} %copy-done.1), custom_call_target="tpu_custom_call" | custom-call | flops 671088640 | bytes 3670016 | tf_op jit(solution)/shard_map/products/pallas_call | solution.py:52
  7.2 0.0 copy-start.2
  7.3 0.0 copy-start.3
  7.3 0.0 copy-start.4
  7.3 0.6 %collective-permute-start = (f32[2,256,256]{2,1,0:T(8,128)S(1)}, f32[2,256,256]{2,1,0:T(8,128)S(1)}, u32[]{:S(2)}, u32[]{:S(2)}) collective-permute-start(f32[2,256,256]{2,1,0:T(8,128)S(1)} %slice_bitcast_fusion.2), channel_id=1, source_target_pairs={{0,1},{1,0},{2,3},{3,2},{4,5},{5,4},{6,7},{7,6},{8,9},{9,8},{10,11... | collective-permute-start | bytes 1572872 | tf_op jit(solution)/shard_map/ppermute | solution.py:17
  7.9 0.0 collective-permute-done.1
  7.9 0.1 fusion.1
  8.0 1.6 %collective-permute-start.2 = (f16[2,256,256]{2,1,0:T(8,128)(2,1)S(1)}, f16[2,256,256]{2,1,0:T(8,128)(2,1)S(1)}, u32[]{:S(2)}, u32[]{:S(2)}) collective-permute-start(f16[2,256,256]{2,1,0:T(8,128)(2,1)S(1)} %fusion.1), channel_id=1, source_target_pairs={{0,2},{1,3},{2,0},{3,1},{4,6},{5,7},{6,4},{7,5},{8,10},{9,11},{10,... | collective-permute-start | bytes 786440 | tf_op jit(solution)/shard_map/ppermute | solution.py:17
  9.6 0.0 collective-permute-done
  9.6 6.7 %collective-permute-done.2 = f16[2,256,256]{2,1,0:T(8,128)(2,1)S(1)} collective-permute-done((f16[2,256,256]{2,1,0:T(8,128)(2,1)S(1)}, f16[2,256,256]{2,1,0:T(8,128)(2,1)S(1)}, u32[]{:S(2)}, u32[]{:S(2)}) %collective-permute-start.2) | collective-permute-done | bytes 262176 | tf_op jit(solution)/shard_map/ppermute | solution.py:17
  16.3 0.1 fusion.4
  16.4 1.6 %collective-permute-start.3 = (f16[2,256,256]{2,1,0:T(8,128)(2,1)S(1)}, f16[2,256,256]{2,1,0:T(8,128)(2,1)S(1)}, u32[]{:S(2)}, u32[]{:S(2)}) collective-permute-start(f16[2,256,256]{2,1,0:T(8,128)(2,1)S(1)} %get-tuple-element.11), channel_id=1, source_target_pairs={{0,4},{4,0},{8,12},{12,8},{16,20},{20,16},{24,28},{28,24},{1,5},{5... | collective-permute-start | bytes 786440 | tf_op jit(solution)/shard_map/ppermute | solution.py:17
  18.0 0.1 pad.3.clone
  18.0 0.0 copy-done.2
  18.0 0.0 copy-done.3
  18.0 0.0 copy-done.4
  18.0 0.1 maximum_maximum_fusion.small_own
  18.1 0.5 %collective-permute-start.4 = (f32[24,256]{1,0:T(8,128)S(1)}, f32[24,256]{1,0:T(8,128)S(1)}, u32[]{:S(2)}, u32[]{:S(2)}) collective-permute-start(f32[24,256]{1,0:T(8,128)S(1)} %maximum_maximum_fusion.small_own), channel_id=1, source_target_pairs={{0,4},{4,0},{8,12},{12,8},{16,20},{20,16},{24,28},{28,24},{1,5},{5... | collective-permute-start | bytes 73736 | tf_op jit(solution)/shard_map/ppermute | solution.py:17
  18.6 5.4 %collective-permute-done.3 = f16[2,256,256]{2,1,0:T(8,128)(2,1)S(1)} collective-permute-done((f16[2,256,256]{2,1,0:T(8,128)(2,1)S(1)}, f16[2,256,256]{2,1,0:T(8,128)(2,1)S(1)}, u32[]{:S(2)}, u32[]{:S(2)}) %collective-permute-start.3) | collective-permute-done | bytes 262176 | tf_op jit(solution)/shard_map/ppermute | solution.py:17
  24.1 0.2 collective-permute-done.4.small_partner
  24.3 1.0 %start.1 = (bf16[4,256,512]{2,1,0:T(8,128)(2,1)S(1)}, f32[2,24,256]{2,1,0:T(8,128)S(1)}, f32[2,2,8,256]{3,2,1,0:T(8,128)S(1)}) custom-call(f32[2,256,256]{2,1,0:T(8,128)S(1)} %get-tuple-element.12.own_ref, f32[2,256,256]{2,1,0:T(8,128)S(1)} %convert_element_type.15.other_ref, f32[24,256]{1,0:T(8,128)S(1)} %maximum_maximum_fusion.small_own, ...), custom_call_target="tpu_custom_call" | custom-call | tf_op jit(solution)/shard_map/start/pallas_call | solution.py:184
  25.4 0.7 %collective-permute-start.5 = (f32[2,8,256]{2,1,0:T(8,128)S(1)}, f32[2,8,256]{2,1,0:T(8,128)S(1)}, u32[]{:S(2)}, u32[]{:S(2)}) collective-permute-start(f32[2,8,256]{2,1,0:T(8,128)S(1)} %slice_bitcast_fusion.6), channel_id=1, source_target_pairs={{0,8},{4,12},{1,9},{5,13},{2,10},{6,14},{3,11},{7,15}} | collective-permute-start | bytes 49160 | tf_op jit(solution)/shard_map/ppermute | solution.py:199
  26.1 0.0 collective-permute-done.5.came
  26.1 0.7 %collective-permute-start.6 = (f32[2,8,256]{2,1,0:T(8,128)S(1)}, f32[2,8,256]{2,1,0:T(8,128)S(1)}, u32[]{:S(2)}, u32[]{:S(2)}) collective-permute-start(f32[2,8,256]{2,1,0:T(8,128)S(1)} %slice_bitcast_fusion.5), channel_id=1, source_target_pairs={{8,16},{12,20},{9,17},{13,21},{10,18},{14,22},{11,19},{15,23}} | collective-permute-start | bytes 49160 | tf_op jit(solution)/shard_map/ppermute | solution.py:199
  26.8 0.0 collective-permute-done.6.came
  26.9 1.3 %collective-permute-start.7 = (f32[2,8,256]{2,1,0:T(8,128)S(1)}, f32[2,8,256]{2,1,0:T(8,128)S(1)}, u32[]{:S(2)}, u32[]{:S(2)}) collective-permute-start(f32[2,8,256]{2,1,0:T(8,128)S(1)} %slice_bitcast_fusion.4), channel_id=1, source_target_pairs={{16,24},{20,28},{17,25},{21,29},{18,26},{22,30},{19,27},{23,31}} | collective-permute-start | bytes 49160 | tf_op jit(solution)/shard_map/ppermute | solution.py:199
  28.2 11.8 %collective-permute-done.7.came = f32[2,8,256]{2,1,0:T(8,128)S(1)} collective-permute-done((f32[2,8,256]{2,1,0:T(8,128)S(1)}, f32[2,8,256]{2,1,0:T(8,128)S(1)}, u32[]{:S(2)}, u32[]{:S(2)}) %collective-permute-start.7) | collective-permute-done | bytes 16416 | tf_op jit(solution)/shard_map/ppermute | solution.py:199
  40.0 1.0 %hop3.1 = f32[2,2,8,256]{3,2,1,0:T(8,128)S(1)} custom-call(bf16[4,256,512]{2,1,0:T(8,128)(2,1)S(1)} %get-tuple-element.8.blocks_ref, f32[2,24,256]{2,1,0:T(8,128)S(1)} %get-tuple-element.9.small_ref, f32[2,8,256]{2,1,0:T(8,128)S(1)} %collective-permute-done.7.came, f32[2,2,8,256]{3,2,1,0:T(8,128)S(1)} %hop2.1.current), custom_call_target="tpu_custom_call" | custom-call | tf_op jit(solution)/shard_map/hop3/pallas_call | solution.py:200
  41.0 0.6 %slice_select_fusion = f32[1,2,8,256]{3,2,1,0:T(8,128)} fusion(f32[2,2,8,256]{3,2,1,0:T(8,128)S(1)} %hop3.1, pred[]{:T(512)S(6)} %eq.3), kind=kLoop, calls=%fused_computation.9 | loop fusion | flops 4096 | bytes 49153 | tf_op jit(solution)/shard_map/jit(_where)/select_n | solution.py:209
  (9 shorter events, 0.2 us)
Async XLA Ops:
  0.0 1.7 %copy-start = (bf16[1,2,1024,640]{3,2,1,0:T(8,128)(2,1)S(1)}, bf16[1,2,1024,640]{3,2,1,0:T(8,128)(2,1)}, u32[]{:S(2)}) copy-start(bf16[1,2,1024,640]{3,2,1,0:T(8,128)(2,1)} %u_hbm.3) | copy-start | bytes 7864324
  1.7 1.7 %copy-start.1 = (bf16[1,2,1024,640]{3,2,1,0:T(8,128)(2,1)S(1)}, bf16[1,2,1024,640]{3,2,1,0:T(8,128)(2,1)}, u32[]{:S(2)}) copy-start(bf16[1,2,1024,640]{3,2,1,0:T(8,128)(2,1)} %vt_hbm.3) | copy-start | bytes 7864324
  5.3 2.5 %collective-permute-start.1 = (f32[2,256,256]{2,1,0:T(8,128)S(1)}, f32[2,256,256]{2,1,0:T(8,128)S(1)}, u32[]{:S(2)}, u32[]{:S(2)}) collective-permute-start(f32[2,256,256]{2,1,0:T(8,128)S(1)} %slice_bitcast_fusion), channel_id=1, source_target_pairs={{0,1},{1,0},{2,3},{3,2},{4,5},{5,4},{6,7},{7,6},{8,9},{9,8},{10,11... | collective-permute-start | bytes 1572872 | tf_op jit(solution)/shard_map/ppermute | solution.py:17
  7.2 10.8 %copy-start.2 = (f32[1,2,8,256]{3,2,1,0:T(8,128)S(1)}, f32[1,2,8,256]{3,2,1,0:T(8,128)}, u32[]{:S(2)}) copy-start(f32[1,2,8,256]{3,2,1,0:T(8,128)} %param.9) | copy-start | bytes 49156
  7.3 10.8 %copy-start.3 = (f32[1,2,256]{2,1,0:T(2,128)S(1)}, f32[1,2,256]{2,1,0:T(2,128)}, u32[]{:S(2)}) copy-start(f32[1,2,256]{2,1,0:T(2,128)} %param.7) | copy-start | bytes 6148
  7.3 10.8 %copy-start.4 = (f32[1,256]{1,0:T(1,128)S(1)}, f32[1,256]{1,0:T(1,128)}, u32[]{:S(2)}) copy-start(f32[1,256]{1,0:T(1,128)} %param.8) | copy-start | bytes 3076
  7.3 2.3 %collective-permute-start = (f32[2,256,256]{2,1,0:T(8,128)S(1)}, f32[2,256,256]{2,1,0:T(8,128)S(1)}, u32[]{:S(2)}, u32[]{:S(2)}) collective-permute-start(f32[2,256,256]{2,1,0:T(8,128)S(1)} %slice_bitcast_fusion.2), channel_id=1, source_target_pairs={{0,1},{1,0},{2,3},{3,2},{4,5},{5,4},{6,7},{7,6},{8,9},{9,8},{10,11... | collective-permute-start | bytes 1572872 | tf_op jit(solution)/shard_map/ppermute | solution.py:17
  8.0 8.3 %collective-permute-start.2 = (f16[2,256,256]{2,1,0:T(8,128)(2,1)S(1)}, f16[2,256,256]{2,1,0:T(8,128)(2,1)S(1)}, u32[]{:S(2)}, u32[]{:S(2)}) collective-permute-start(f16[2,256,256]{2,1,0:T(8,128)(2,1)S(1)} %fusion.1), channel_id=1, source_target_pairs={{0,2},{1,3},{2,0},{3,1},{4,6},{5,7},{6,4},{7,5},{8,10},{9,11},{10,... | collective-permute-start | bytes 786440 | tf_op jit(solution)/shard_map/ppermute | solution.py:17
  16.4 7.7 %collective-permute-start.3 = (f16[2,256,256]{2,1,0:T(8,128)(2,1)S(1)}, f16[2,256,256]{2,1,0:T(8,128)(2,1)S(1)}, u32[]{:S(2)}, u32[]{:S(2)}) collective-permute-start(f16[2,256,256]{2,1,0:T(8,128)(2,1)S(1)} %get-tuple-element.11), channel_id=1, source_target_pairs={{0,4},{4,0},{8,12},{12,8},{16,20},{20,16},{24,28},{28,24},{1,5},{5... | collective-permute-start | bytes 786440 | tf_op jit(solution)/shard_map/ppermute | solution.py:17
  18.1 6.2 %collective-permute-start.4 = (f32[24,256]{1,0:T(8,128)S(1)}, f32[24,256]{1,0:T(8,128)S(1)}, u32[]{:S(2)}, u32[]{:S(2)}) collective-permute-start(f32[24,256]{1,0:T(8,128)S(1)} %maximum_maximum_fusion.small_own), channel_id=1, source_target_pairs={{0,4},{4,0},{8,12},{12,8},{16,20},{20,16},{24,28},{28,24},{1,5},{5... | collective-permute-start | bytes 73736 | tf_op jit(solution)/shard_map/ppermute | solution.py:17
  25.4 0.7 %collective-permute-start.5 = (f32[2,8,256]{2,1,0:T(8,128)S(1)}, f32[2,8,256]{2,1,0:T(8,128)S(1)}, u32[]{:S(2)}, u32[]{:S(2)}) collective-permute-start(f32[2,8,256]{2,1,0:T(8,128)S(1)} %slice_bitcast_fusion.6), channel_id=1, source_target_pairs={{0,8},{4,12},{1,9},{5,13},{2,10},{6,14},{3,11},{7,15}} | collective-permute-start | bytes 49160 | tf_op jit(solution)/shard_map/ppermute | solution.py:199
  26.1 0.7 %collective-permute-start.6 = (f32[2,8,256]{2,1,0:T(8,128)S(1)}, f32[2,8,256]{2,1,0:T(8,128)S(1)}, u32[]{:S(2)}, u32[]{:S(2)}) collective-permute-start(f32[2,8,256]{2,1,0:T(8,128)S(1)} %slice_bitcast_fusion.5), channel_id=1, source_target_pairs={{8,16},{12,20},{9,17},{13,21},{10,18},{14,22},{11,19},{15,23}} | collective-permute-start | bytes 49160 | tf_op jit(solution)/shard_map/ppermute | solution.py:199
  26.9 13.1 %collective-permute-start.7 = (f32[2,8,256]{2,1,0:T(8,128)S(1)}, f32[2,8,256]{2,1,0:T(8,128)S(1)}, u32[]{:S(2)}, u32[]{:S(2)}) collective-permute-start(f32[2,8,256]{2,1,0:T(8,128)S(1)} %slice_bitcast_fusion.4), channel_id=1, source_target_pairs={{16,24},{20,28},{17,25},{21,29},{18,26},{22,30},{19,27},{23,31}} | collective-permute-start | bytes 49160 | tf_op jit(solution)/shard_map/ppermute | solution.py:199
